TPU v7x, 32 devices: a whole 2x2x4 slice. The times are simulated.
32 devices in a mesh: patch: 8 (over z, y), sample: 4 (over x, core).
Axes of the slice: x: 2, y: 2, z: 4, core: 2. Of those that a mesh axis runs over, the one named last changes fastest.
Arguments:
- features: bfloat16 [4, 4096, 512], P('sample', 'patch'), may hold values from -600 to 600
- cotangent: bfloat16 [4, 4096, 512], P('sample', 'patch'), may hold values from -6 to 6
- weight_qkv: bfloat16 [512, 1536], replicated, may hold values from -5 to 5
- weight_out: bfloat16 [512, 512], replicated, may hold values from -0.25 to 0.25
- key_tiles: int32 [32, 8], replicated, may hold values from 0 to 31, as said below
- tile_valid: int32 [32, 8], replicated, may hold values from 0 to 1, as said below
Outputs:
- grad_features: bfloat16 [4, 4096, 512], P('sample', 'patch')
- grad_qkv: float32 [512, 1536], replicated
- grad_out: float32 [512, 512], replicated
Inputs may be any that keep to these rules, and one draw needn't show every extreme that they name: `key_tiles`: row g names 8 distinct tile ids. A tile's patch is its id // 4. The first id is g itself, the next 3 are other tiles of g's patch, and the last 4 lie one each in the patches at offsets -2 to 2 other than 0 around the cycle of patches, in rising order of offset. Over the rows of one patch exactly 2 distinct tiles of each such neighbouring patch are named. `tile_valid`: column 0 is always 1.
All inputs are finite; a program needn't handle non-finite values.
Results may differ from a plain program's by a relative error of at most 0.0088.
Values may be sent and summed in bfloat16 or wider, within the bound.
No kernel may reach another device: no remote copies, remote signals or barrier semaphores. Data moves between devices by JAX's collectives and lax.ppermute only.
A program may use at most 192 MiB of HBM per device.

v0:
```python
from functools import partial
import math
import jax
import jax.numpy as jnp
from jax import lax
from jax.sharding import PartitionSpec as P

HEADS = 4
TILE = 128
NB = 8
REACH = 2
CAP = 2
epsilon = 1e-06


def from_behind(value, axis, steps):
    count = lax.axis_size(axis)
    pairs = [(source, (source + steps) % count) for source in range(count)]
    return lax.ppermute(value, axis, pairs)


def tile_backward(query_tile, pair_tiles, live_flags, grad_tile, head_count):
    row_count = query_tile.shape[0]
    model_width = query_tile.shape[1]
    head_width = model_width // head_count
    scaling = head_width ** (-0.5)
    key_heads = pair_tiles[:, :, :model_width].reshape(-1, head_count, head_width)
    value_heads = pair_tiles[:, :, model_width:].reshape(-1, head_count, head_width)
    query_heads = query_tile.reshape(row_count, head_count, head_width)
    grad_heads = grad_tile.reshape(row_count, head_count, head_width)
    scores = (
        jnp.einsum("qhd,khd->hqk", query_heads, key_heads, preferred_element_type=jnp.float32)
        * scaling
    )
    live_mask = jnp.repeat(live_flags > 0, pair_tiles.shape[1])
    scores = jnp.where(live_mask[None, None, :], scores, -jnp.inf)
    highest = jnp.max(scores, -1, keepdims=True)
    expanded = jnp.exp(scores - highest)
    attention = expanded / jnp.sum(expanded, -1, keepdims=True)
    attention_low = attention.astype(jnp.bfloat16)
    attended = jnp.einsum(
        "hqk,khd->qhd", attention_low, value_heads, preferred_element_type=jnp.float32
    )
    attended = attended.astype(jnp.bfloat16).reshape(row_count, model_width)
    dprob = jnp.einsum("qhd,khd->hqk", grad_heads, value_heads, preferred_element_type=jnp.float32)
    centre = jnp.sum(attention * dprob, -1, keepdims=True)
    dscore = (attention * (dprob - centre) * scaling).astype(jnp.bfloat16)
    dquery = jnp.einsum(
        "hqk,khd->qhd", dscore, key_heads, preferred_element_type=jnp.float32
    ).reshape(row_count, model_width)
    dkey = jnp.einsum("hqk,qhd->khd", dscore, query_heads, preferred_element_type=jnp.float32)
    dvalue = jnp.einsum(
        "hqk,qhd->khd", attention_low, grad_heads, preferred_element_type=jnp.float32
    )
    dkey = dkey.reshape(pair_tiles.shape[0], pair_tiles.shape[1], model_width)
    dvalue = dvalue.reshape(pair_tiles.shape[0], pair_tiles.shape[1], model_width)
    return (attended, dquery, jnp.concatenate([dkey, dvalue], -1))


def tile_flags(list_rows, source, tile_count):
    first_id = source * tile_count
    wanted = (
        list_rows[:, :, None] == first_id + jnp.arange(tile_count, dtype=jnp.int32)[None, None, :]
    )
    wanted_flags = jnp.any(wanted, axis=(0, 1))
    wanted_places = jnp.cumsum(wanted_flags.astype(jnp.int32)) - 1
    return (wanted_flags, wanted_places)


def on_device(features, cotangent, weight_qkv, weight_out, key_tiles, tile_valid):
    patches = lax.axis_size("patch")
    position = lax.axis_index("patch")
    rows_local = features.shape[1]
    model_width = features.shape[2]
    tile_count = rows_local // TILE
    offsets = [shift_by for shift_by in range(-REACH, REACH + 1) if shift_by != 0]
    inputs = features[0].astype(jnp.float32)
    inverse = lax.rsqrt(jnp.mean(inputs * inputs, -1, keepdims=True) + epsilon)
    normed = inputs * inverse
    normed_low = normed.astype(jnp.bfloat16)
    projected = jnp.dot(normed_low, weight_qkv, preferred_element_type=jnp.float32).astype(
        jnp.bfloat16
    )
    queries = projected[:, :model_width]
    pairs_own = projected[:, model_width:].reshape(tile_count, TILE, 2 * model_width)
    grad_rows = cotangent[0]
    grad_attended = jnp.einsum(
        "pe,de->pd", grad_rows, weight_out, preferred_element_type=jnp.float32
    ).astype(jnp.bfloat16)
    my_lists = lax.dynamic_slice_in_dim(key_tiles, position * tile_count, tile_count, 0)
    my_valid = lax.dynamic_slice_in_dim(tile_valid, position * tile_count, tile_count, 0)
    owner_patch = my_lists // tile_count
    within = my_lists % tile_count
    distance = (owner_patch - position) % patches
    distance = jnp.where(distance > patches // 2, distance - patches, distance)
    order_index = jnp.where(distance < 0, distance + REACH, distance + REACH - 1)
    senders = []
    tile_range = jnp.arange(tile_count, dtype=jnp.int32)
    arrivals = []
    place_rows = []
    for shift_by in offsets:
        target = (position - shift_by) % patches
        target_lists = lax.dynamic_slice_in_dim(key_tiles, target * tile_count, tile_count, 0)
        wanted_flags, wanted_places = tile_flags(target_lists, position, tile_count)
        picker = wanted_flags[None, :] & (
            wanted_places[None, :] == jnp.arange(CAP, dtype=jnp.int32)[:, None]
        )
        send_rows = jnp.sum(jnp.where(picker, tile_range[None, :], 0), 1)
        senders.append(send_rows)
        packed = jnp.take(pairs_own, send_rows, axis=0)
        arrived = from_behind(packed, "patch", -shift_by)
        arrivals.append(arrived)
        source = (position + shift_by) % patches
        incoming_flags, incoming_places = tile_flags(my_lists, source, tile_count)
        place_rows.append(incoming_places)
    buffer = jnp.concatenate([pairs_own] + arrivals, 0)
    place_table = jnp.concatenate(place_rows, 0)
    lookup = order_index * tile_count + within
    matched = lookup[:, :, None] == jnp.arange(place_table.shape[0], dtype=jnp.int32)[None, None, :]
    remote_place = jnp.sum(jnp.where(matched, place_table[None, None, :], 0), -1)
    slot_ids = jnp.where(distance == 0, within, tile_count + order_index * CAP + remote_place)
    group_size = math.gcd(4, tile_count)
    step_count = tile_count // group_size
    tile_pass = jax.vmap(partial(tile_backward, head_count=HEADS))
    buffer_count = buffer.shape[0]

    def advance(running, pieces):
        query_group, slot_group, live_group, grad_group = pieces
        flat_slots = slot_group.reshape(-1)
        gathered = jnp.take(buffer, flat_slots, axis=0).reshape(
            group_size, NB, TILE, 2 * model_width
        )
        attended, dquery, dpairs = tile_pass(query_group, gathered, live_group, grad_group)
        running = running.at[flat_slots].add(dpairs.reshape(group_size * NB, TILE, 2 * model_width))
        return (running, (attended, dquery))

    start_sums = jnp.zeros((buffer_count, TILE, 2 * model_width), jnp.float32)
    scanned = (
        queries.reshape(step_count, group_size, TILE, model_width),
        slot_ids.reshape(step_count, group_size, NB),
        my_valid.reshape(step_count, group_size, NB),
        grad_attended.reshape(step_count, group_size, TILE, model_width),
    )
    totals, (attended_all, dquery_all) = lax.scan(advance, start_sums, scanned)
    grads_own = totals[:tile_count]
    for offset_index, shift_by in enumerate(offsets):
        portion = totals[tile_count + offset_index * CAP : tile_count + (offset_index + 1) * CAP]
        returned = from_behind(portion.astype(jnp.bfloat16), "patch", shift_by).astype(
            portion.dtype
        )
        grads_own = grads_own.at[senders[offset_index]].add(returned)
    attended_rows = attended_all.reshape(rows_local, model_width)
    grad_projected = jnp.concatenate(
        [
            dquery_all.reshape(rows_local, model_width),
            grads_own.reshape(rows_local, 2 * model_width),
        ],
        1,
    ).astype(jnp.bfloat16)
    grad_normed = jnp.einsum(
        "pe,de->pd", grad_projected, weight_qkv, preferred_element_type=jnp.float32
    )
    grad_inputs = grad_rows.astype(jnp.float32) + inverse * (
        grad_normed - normed * jnp.mean(grad_normed * normed, -1, keepdims=True)
    )
    local_qkv = jnp.einsum(
        "pd,pe->de", normed_low, grad_projected, preferred_element_type=jnp.float32
    )
    local_out = jnp.einsum(
        "pd,pe->de", attended_rows, grad_rows, preferred_element_type=jnp.float32
    )
    summed_qkv, summed_out = lax.psum((local_qkv, local_out), ("patch", "sample"))
    factor = float(lax.axis_size("patch") * lax.axis_size("sample") * rows_local) ** (-0.5)
    return (grad_inputs.astype(jnp.bfloat16)[None], summed_qkv * factor, summed_out * factor)


def solution(mesh):
    placed = (P("sample", "patch", None), P("sample", "patch", None), P(), P(), P(), P())
    return jax.shard_map(
        on_device,
        mesh=mesh,
        in_specs=placed,
        out_specs=(P("sample", "patch", None), P(), P()),
        check_vma=False,
    )
```

profile of v0, /device:TPU:0, one launch (start us, length us, event | category | flops | bytes accessed | tf_op | source)
XLA Modules:
  0.0 484.2 jit_solution(8484835399230841525)
XLA Ops:
  16.4 5.1 %collective-permute-start.3 = (bf16[2,128,1024]{2,1,0:T(8,128)(2,1)}, bf16[2,128,1024]{2,1,0:T(8,128)(2,1)}, u32[]{:S(2)}, u32[]{:S(2)}) collective-permute-start(bf16[2,128,1024]{2,1,0:T(8,128)(2,1)} %broadcast_select_fusion.1), channel_id=1, source_target_pairs={{0,24},{4,28},{8,0},{12,4},{16,8},{20,12},{24,16},{28,20},{1,25},{... | collective-permute-start | bytes 1572872 | tf_op jit(solution)/shard_map/ppermute | solution.py:19
  50.4 6.0 %collective-permute-done = bf16[2,128,1024]{2,1,0:T(8,128)(2,1)} collective-permute-done((bf16[2,128,1024]{2,1,0:T(8,128)(2,1)}, bf16[2,128,1024]{2,1,0:T(8,128)(2,1)}, u32[]{:S(2)}, u32[]{:S(2)}) %collective-permute-start) | collective-permute-done | bytes 524320 | tf_op jit(solution)/shard_map/ppermute | solution.py:19
  63.9 7.0 %gather_fusion = bf16[32,128,1024]{2,1,0:T(8,128)(2,1)} fusion(bf16[12,128,1024]{2,1,0:T(8,128)(2,1)} %constant_dynamic-update-slice_fusion, s32[1024]{0:T(1024)S(1)} %pad_clamp_fusion), kind=kCustom, calls=%fused_computation.4 | custom fusion | bytes 16777344 | tf_op jit(solution)/shard_map/while/body/eval_jaxpr/jit(_take)/gather | solution.py:130
  70.9 7.5 %broadcast_select_fusion = bf16[4,8,128,1024]{3,2,1,0:T(8,128)(2,1)} fusion(bf16[4,8,128,1024]{3,2,1,0:T(8,128)(2,1)} %bitcast.111, pred[4,8]{1,0:T(4,128)(4,1)S(1)} %get-tuple-element.53), kind=kLoop, calls=%fused_computation.18 | loop fusion | flops 4194304 | bytes 16777248 | tf_op jit(solution)/shard_map/while/body/eval_jaxpr/jit(_take)/select_n | solution.py:130
  78.4 5.9 %fusion.74 = (bf16[4,8,128,512]{3,2,1,0:T(8,128)(2,1)}, bf16[4,8,128,512]{3,2,1,0:T(8,128)(2,1)}) fusion(bf16[4,8,128,1024]{3,2,1,0:T(8,128)(2,1)} %broadcast_select_fusion), kind=kLoop, calls=%fused_computation.171 | loop fusion | bytes 16777216 | tf_op jit(solution)/shard_map/while/body/eval_jaxpr/vmap()/slice | solution.py:28
  84.2 6.9 %reshape.576 = bf16[4,1024,4,128]{3,2,1,0:T(4,128)(2,1)} reshape(bf16[4,8,128,512]{3,2,1,0:T(8,128)(2,1)} %get-tuple-element.56) | data formatting | bytes 8388608 | tf_op jit(solution)/shard_map/while/body/eval_jaxpr/vmap()/reshape | solution.py:27
  91.2 7.5 %copy.96 = bf16[4,1024,4,128]{1,3,2,0:T(8,128)(2,1)} copy(bf16[4,1024,4,128]{3,2,1,0:T(4,128)(2,1)} %reshape.576) | data formatting | bytes 8388608 | tf_op jit(solution)/shard_map/while/body/eval_jaxpr/vmap()/reshape | solution.py:27
  98.7 6.9 %reshape.577 = bf16[4,1024,4,128]{3,2,1,0:T(4,128)(2,1)} reshape(bf16[4,8,128,512]{3,2,1,0:T(8,128)(2,1)} %get-tuple-element.55) | data formatting | bytes 8388608 | tf_op jit(solution)/shard_map/while/body/eval_jaxpr/vmap()/reshape | solution.py:28
  105.6 7.6 %copy.95 = bf16[4,1024,4,128]{1,3,2,0:T(8,128)(2,1)} copy(bf16[4,1024,4,128]{3,2,1,0:T(4,128)(2,1)} %reshape.577) | data formatting | bytes 8388608 | tf_op jit(solution)/shard_map/while/body/eval_jaxpr/vmap()/reshape | solution.py:28
  113.2 6.8 %fusion.77 = f32[4,4,128,1024]{3,2,1,0:T(8,128)} fusion(bf16[4,128,4,128]{1,3,2,0:T(8,128)(2,1)S(1)} %copy-done.3, bf16[4,1024,4,128]{1,3,2,0:T(8,128)(2,1)} %copy.95), kind=kOutput, calls=%fused_computation.174 | convolution fusion | flops 536870912 | bytes 13107200 | tf_op jit(solution)/shard_map/while/body/eval_jaxpr/vmap(qhd,khd->hqk)/dot_general | solution.py:45
  120.0 8.5 %fusion.76 = (f32[4,4,128]{2,1,0:T(4,128)S(1)}, f32[4,4,128,1024]{3,2,1,0:T(8,128)}) fusion(pred[4,1024]{1,0:T(4,128)(4,1)S(1)} %bitcast.123, bf16[4,128,4,128]{1,3,2,0:T(8,128)(2,1)S(1)} %copy-done.7, bf16[4,1024,4,128]{1,3,2,0:T(8,128)(2,1)} %copy.96), kind=kOutput, calls=%fused_computation.173 | convolution fusion | flops 545260544 | bytes 13119488 | tf_op jit(solution)/shard_map/while/body/eval_jaxpr/vmap()/sub | solution.py:38
  128.5 6.9 %fusion.30 = bf16[4,128,4,128]{1,3,2,0:T(8,128)(2,1)} fusion(bf16[4,1024,4,128]{1,3,2,0:T(8,128)(2,1)} %copy.95, f32[4,4,128,1024]{3,2,1,0:T(8,128)} %get-tuple-element.67, f32[4,4,128]{2,1,0:T(4,128)S(1)} %get-tuple-element.66), kind=kOutput, calls=%fused_computation.42 | convolution fusion | flops 541327360 | bytes 13115392 | tf_op jit(solution)/shard_map/while/body/eval_jaxpr/vmap(hqk,khd->qhd)/dot_general | solution.py:41
  135.5 4.0 convolution_bitcast_fusion
  139.6 23.7 %fusion.15 = f32[4,1024,4,128]{1,3,2,0:T(8,128)} fusion(bf16[4,128,4,128]{1,3,2,0:T(8,128)(2,1)S(1)} %copy-done.7, f32[4,4,128,1024]{3,2,1,0:T(8,128)} %fusion.77, f32[4,4,128,1024]{3,2,1,0:T(8,128)} %get-tuple-element.67, f32[4,4,128]{2,1,0:T(4,128)S(1)} %get-tuple-element.66), kind=kOutput, calls=%fused_computation.26 | convolution fusion | flops 551554048 | bytes 25698304 | tf_op jit(solution)/shard_map/while/body/eval_jaxpr/vmap(hqk,qhd->khd)/dot_general | solution.py:51
  163.3 9.9 %copy.89 = f32[4,1024,4,128]{3,2,1,0:T(4,128)} copy(f32[4,1024,4,128]{1,3,2,0:T(8,128)} %fusion.15) | data formatting | bytes 16777216 | tf_op jit(solution)/shard_map/while/body/eval_jaxpr/vmap(hqk,qhd->khd)/transpose | solution.py:51
  173.2 10.3 %concatenate.21 = f32[32,128,512]{2,1,0:T(8,128)} reshape(f32[4,1024,4,128]{3,2,1,0:T(4,128)} %copy.89) | data formatting | bytes 16777216 | tf_op jit(solution)/shard_map/while/body/eval_jaxpr/vmap()/concatenate | solution.py:57
  183.4 9.9 %copy.91 = f32[4,1024,4,128]{3,2,1,0:T(4,128)} copy(f32[4,1024,4,128]{1,3,2,0:T(8,128)} %convolution_bitcast_fusion) | data formatting | bytes 16777216 | tf_op jit(solution)/shard_map/while/body/eval_jaxpr/vmap(hqk,qhd->khd)/transpose | solution.py:52
  193.3 10.3 %concatenate.22 = f32[32,128,512]{2,1,0:T(8,128)} reshape(f32[4,1024,4,128]{3,2,1,0:T(4,128)} %copy.91) | data formatting | bytes 16777216 | tf_op jit(solution)/shard_map/while/body/eval_jaxpr/vmap()/concatenate | solution.py:57
  203.6 11.7 %pad_maximum_fusion = f32[32,128,1024]{2,1,0:T(8,128)} fusion(f32[32,128,512]{2,1,0:T(8,128)} %concatenate.22, f32[32,128,512]{2,1,0:T(8,128)} %concatenate.21), kind=kLoop, calls=%fused_computation.12 | loop fusion | flops 4194304 | bytes 33554432 | tf_op jit(solution)/shard_map/while/body/eval_jaxpr/vmap()/concatenate | solution.py:57
  218.7 35.9 %scatter_fusion = f32[12,128,1024]{2,1,0:T(8,128)} fusion(f32[12,128,1024]{2,1,0:T(8,128)} %broadcast_in_dim.161, s32[32]{0:T(128)S(1)} %fusion.61, f32[32,128,1024]{2,1,0:T(8,128)} %pad_maximum_fusion), kind=kCustom, calls=%fused_computation.5 | custom fusion | flops 4194304 | bytes 50331776 | tf_op jit(solution)/shard_map/while/body/eval_jaxpr/scatter-add | solution.py:134
  254.6 4.9 %convert.25 = bf16[12,128,1024]{2,1,0:T(8,128)(2,1)} convert(f32[12,128,1024]{2,1,0:T(8,128)} %scatter_fusion) | non-fusion elementwise | flops 1572864 | bytes 9437184 | tf_op jit(solution)/shard_map/convert.17
  273.1 22.8 %fusion.33 = bf16[4,128,4,128]{1,3,2,0:T(8,128)(2,1)S(1)} fusion(bf16[4,1024,4,128]{1,3,2,0:T(8,128)(2,1)} %copy.96, f32[4,4,128,1024]{3,2,1,0:T(8,128)} %fusion.77, f32[4,4,128,1024]{3,2,1,0:T(8,128)} %get-tuple-element.67, f32[4,4,128]{2,1,0:T(4,128)S(1)} %get-tuple-element.66), kind=kOutput, calls=%fused_computation.43 | convolution fusion | flops 551816192 | bytes 21504000 | tf_op jit(solution)/shard_map/while/body/eval_jaxpr/vmap(hqk,khd->qhd)/dot_general | solution.py:48
  332.9 139.6 %all-reduce.3.cloned.1.call-done = (f32[512,1536]{1,0:T(8,128)}, f32[512,512]{1,0:T(8,128)}) async-done(((f32[512,1536]{1,0:T(8,128)}, f32[512,512]{1,0:T(8,128)}), (f32[512,1536]{1,0:T(8,128)}, f32[512,512]{1,0:T(8,128)})) %all-reduce.3.cloned.1.call-update) | async-done | bytes 4194320 | tf_op jit(solution)/shard_map/psum | solution.py:172
  472.4 3.9 broadcast_multiply_fusion
  (150 shorter events, 100.2 us)
Async XLA Ops:
  7.2 3.7 copy-start
  7.2 465.2 %all-reduce.3.cloned.1.call-start = ((), (), s32[]{:S(2)}) async-start(), calls=%async_computation | async-start | bytes 8388608 | tf_op jit(solution)/shard_map/psum | solution.py:172
  11.9 1.1 copy-start.5
  13.1 23.5 %copy-start.9 = (s32[32,8]{0,1:T(8,128)S(1)}, s32[32,8]{0,1:T(8,128)}, u32[]{:S(2)}) copy-start(s32[32,8]{0,1:T(8,128)} %param.13) | copy-start | bytes 3076
  16.4 45.6 %collective-permute-start.3 = (bf16[2,128,1024]{2,1,0:T(8,128)(2,1)}, bf16[2,128,1024]{2,1,0:T(8,128)(2,1)}, u32[]{:S(2)}, u32[]{:S(2)}) collective-permute-start(bf16[2,128,1024]{2,1,0:T(8,128)(2,1)} %broadcast_select_fusion.1), channel_id=1, source_target_pairs={{0,24},{4,28},{8,0},{12,4},{16,8},{20,12},{24,16},{28,20},{1,25},{... | collective-permute-start | bytes 1572872 | tf_op jit(solution)/shard_map/ppermute | solution.py:19
  24.9 35.3 %collective-permute-start.2 = (bf16[2,128,1024]{2,1,0:T(8,128)(2,1)}, bf16[2,128,1024]{2,1,0:T(8,128)(2,1)}, u32[]{:S(2)}, u32[]{:S(2)}) collective-permute-start(bf16[2,128,1024]{2,1,0:T(8,128)(2,1)} %broadcast_select_fusion.2), channel_id=1, source_target_pairs={{0,28},{4,0},{8,4},{12,8},{16,12},{20,16},{24,20},{28,24},{1,29},{... | collective-permute-start | bytes 1572872 | tf_op jit(solution)/shard_map/ppermute | solution.py:19
  30.2 28.1 %collective-permute-start.1 = (bf16[2,128,1024]{2,1,0:T(8,128)(2,1)}, bf16[2,128,1024]{2,1,0:T(8,128)(2,1)}, u32[]{:S(2)}, u32[]{:S(2)}) collective-permute-start(bf16[2,128,1024]{2,1,0:T(8,128)(2,1)} %broadcast_select_fusion.3), channel_id=1, source_target_pairs={{0,4},{4,8},{8,12},{12,16},{16,20},{20,24},{24,28},{28,0},{1,5},{5... | collective-permute-start | bytes 1572872 | tf_op jit(solution)/shard_map/ppermute | solution.py:19
  34.2 22.3 %collective-permute-start = (bf16[2,128,1024]{2,1,0:T(8,128)(2,1)}, bf16[2,128,1024]{2,1,0:T(8,128)(2,1)}, u32[]{:S(2)}, u32[]{:S(2)}) collective-permute-start(bf16[2,128,1024]{2,1,0:T(8,128)(2,1)} %broadcast_select_fusion.4), channel_id=1, source_target_pairs={{0,8},{4,12},{8,16},{12,20},{16,24},{20,28},{24,0},{28,4},{1,9},{5... | collective-permute-start | bytes 1572872 | tf_op jit(solution)/shard_map/ppermute | solution.py:19
  105.6 7.6 %copy-start.3 = (bf16[4,128,4,128]{1,3,2,0:T(8,128)(2,1)S(1)}, bf16[4,128,4,128]{1,3,2,0:T(8,128)(2,1)}, u32[]{:S(2)}) copy-start(bf16[4,128,4,128]{1,3,2,0:T(8,128)(2,1)} %copy.90) | copy-start | bytes 1572868
  113.2 6.8 %copy-start.7 = (bf16[4,128,4,128]{1,3,2,0:T(8,128)(2,1)S(1)}, bf16[4,128,4,128]{1,3,2,0:T(8,128)(2,1)}, u32[]{:S(2)}) copy-start(bf16[4,128,4,128]{1,3,2,0:T(8,128)(2,1)} %copy.88) | copy-start | bytes 1572868
  128.5 7.0 %copy-start.10 = (f32[4,4,128,1024]{3,2,1,0:T(8,128)S(1)}, f32[4,4,128,1024]{3,2,1,0:T(8,128)}, u32[]{:S(2)}) copy-start(f32[4,4,128,1024]{3,2,1,0:T(8,128)} %get-tuple-element.67) | copy-start | bytes 25165828
  259.6 3.2 copy-start.8
  266.8 33.9 %collective-permute-start.4 = (bf16[2,128,1024]{2,1,0:T(8,128)(2,1)}, bf16[2,128,1024]{2,1,0:T(8,128)(2,1)}, u32[]{:S(2)}, u32[]{:S(2)}) collective-permute-start(bf16[2,128,1024]{2,1,0:T(8,128)(2,1)} %get-tuple-element.60), channel_id=1, source_target_pairs={{0,24},{4,28},{8,0},{12,4},{16,8},{20,12},{24,16},{28,20},{1,25},{... | collective-permute-start | bytes 1572872 | tf_op jit(solution)/shard_map/ppermute | solution.py:19
  270.1 36.1 %collective-permute-start.5 = (bf16[2,128,1024]{2,1,0:T(8,128)(2,1)}, bf16[2,128,1024]{2,1,0:T(8,128)(2,1)}, u32[]{:S(2)}, u32[]{:S(2)}) collective-permute-start(bf16[2,128,1024]{2,1,0:T(8,128)(2,1)} %get-tuple-element.59), channel_id=1, source_target_pairs={{0,28},{4,0},{8,4},{12,8},{16,12},{20,16},{24,20},{28,24},{1,29},{... | collective-permute-start | bytes 1572872 | tf_op jit(solution)/shard_map/ppermute | solution.py:19
  271.6 40.1 %collective-permute-start.6 = (bf16[2,128,1024]{2,1,0:T(8,128)(2,1)}, bf16[2,128,1024]{2,1,0:T(8,128)(2,1)}, u32[]{:S(2)}, u32[]{:S(2)}) collective-permute-start(bf16[2,128,1024]{2,1,0:T(8,128)(2,1)} %get-tuple-element.58), channel_id=1, source_target_pairs={{0,4},{4,8},{8,12},{12,16},{16,20},{20,24},{24,28},{28,0},{1,5},{5... | collective-permute-start | bytes 1572872 | tf_op jit(solution)/shard_map/ppermute | solution.py:19
  272.1 26.1 %copy-start.1 = (bf16[1,512,512]{2,1,0:T(8,128)(2,1)S(1)}, bf16[1,512,512]{2,1,0:T(8,128)(2,1)}, u32[]{:S(2)}) copy-start(bf16[1,512,512]{2,1,0:T(8,128)(2,1)} %param.9) | copy-start | bytes 1572868
  272.1 45.2 %collective-permute-start.7 = (bf16[2,128,1024]{2,1,0:T(8,128)(2,1)}, bf16[2,128,1024]{2,1,0:T(8,128)(2,1)}, u32[]{:S(2)}, u32[]{:S(2)}) collective-permute-start(bf16[2,128,1024]{2,1,0:T(8,128)(2,1)} %get-tuple-element.57), channel_id=1, source_target_pairs={{0,8},{4,12},{8,16},{12,20},{16,24},{20,28},{24,0},{28,4},{1,9},{5... | collective-permute-start | bytes 1572872 | tf_op jit(solution)/shard_map/ppermute | solution.py:19
  324.6 1.0 copy-start.2
  329.2 2.3 copy-start.4
  472.4 3.9 copy-start.6
Sparse Core Ops, SparseCore 0:
  328.3 144.0 all-reduce.2
where the time goes:
time: 487 us; the launch traced here: 484 us
  waiting for transfers between devices  146 us (30%)
  local copies, waits for them, and re-layouts  126 us (26%)
  other arithmetic  99.9 us (21%)
  matrix products  83.7 us (17%)
  starting transfers between devices  14.5 us (3%)
  between operations  14.4 us (3%)
    psum x1, waiting for transfers between devices, on_device(): lax.psum((local_qkv, local_out), ('patch', 'sample'))  140 us
    scatter-add x1, other arithmetic, advance(): running.at[flat_slots]  35.9 us
    dot_general x1, matrix products, tile_backward(): jnp.einsum('hqk,qhd->khd', dscore, query_heads, preferred_element_type=jn...  23.7 us
    dot_general x1, matrix products, tile_backward(): jnp.einsum('hqk,khd->qhd', dscore, key_heads, preferred_element_type=jnp....  22.8 us
    concatenate x2, local copies, waits for them, and re-layouts, tile_backward(): return (attended, dquery, jnp.concatenate([dkey, dvalue], -1))  20.5 us
    reshape x2, local copies, waits for them, and re-layouts, tile_backward(): pair_tiles[:, :, model_width:].reshape(-1, head_count, head_width)  14.5 us
    reshape x2, local copies, waits for them, and re-layouts, tile_backward(): pair_tiles[:, :, :model_width].reshape(-1, head_count, head_width)  14.4 us
    ppermute x8, starting transfers between devices, from_behind(): return lax.ppermute(value, axis, pairs)  14.4 us
  transfers between devices with their start and end apart: 9, of which 2 were waited for; matrix products, arithmetic and copies ran while one was open for 17% of the time, Pallas kernels for 0%

commit v1 on v0

--- a/solution.py
+++ b/solution.py
@@ -169,7 +169,9 @@
     local_out = jnp.einsum(
         "pd,pe->de", attended_rows, grad_rows, preferred_element_type=jnp.float32
     )
-    summed_qkv, summed_out = lax.psum((local_qkv, local_out), ("patch", "sample"))
+    summed_qkv, summed_out = lax.psum(
+        lax.psum((local_qkv, local_out), axis_name="sample"), axis_name="patch"
+    )
     factor = float(lax.axis_size("patch") * lax.axis_size("sample") * rows_local) ** (-0.5)
     return (grad_inputs.astype(jnp.bfloat16)[None], summed_qkv * factor, summed_out * factor)
 

time: 487 us -> 590 us (1.21)
  waiting for transfers between devices: 146 us -> 249 us
    psum x1 -> x2, waiting for transfers between devices: 140 us -> 243 us  [the longest x1 156 us: on_device(): lax.psum(lax.psum((local_qkv, local_out), axis_name='sample'), axis_name=...]
  transfers between devices with their start and end apart: 9 -> 10, of which waited for: 2 -> 3; matrix products, arithmetic and copies ran while one was open for 17% -> 14% of each run, Pallas kernels for 0% -> 0%
where the time goes in v1:
time: 590 us; the launch traced here: 587 us
  waiting for transfers between devices  249 us (42%)
  local copies, waits for them, and re-layouts  126 us (21%)
  other arithmetic  99.9 us (17%)
  matrix products  83.7 us (14%)
  starting transfers between devices  14.5 us (2%)
  between operations  14.4 us (2%)
    psum x1, waiting for transfers between devices, on_device(): lax.psum(lax.psum((local_qkv, local_out), axis_name='sample'), axis_name=...  156 us
    psum x1, waiting for transfers between devices, on_device(): lax.psum((local_qkv, local_out), axis_name='sample')  87 us
    scatter-add x1, other arithmetic, advance(): running.at[flat_slots]  35.9 us
    dot_general x1, matrix products, tile_backward(): jnp.einsum('hqk,qhd->khd', dscore, query_heads, preferred_element_type=jn...  23.7 us
    dot_general x1, matrix products, tile_backward(): jnp.einsum('hqk,khd->qhd', dscore, key_heads, preferred_element_type=jnp....  22.8 us
    concatenate x2, local copies, waits for them, and re-layouts, tile_backward(): return (attended, dquery, jnp.concatenate([dkey, dvalue], -1))  20.5 us
    reshape x2, local copies, waits for them, and re-layouts, tile_backward(): pair_tiles[:, :, model_width:].reshape(-1, head_count, head_width)  14.5 us
    reshape x2, local copies, waits for them, and re-layouts, tile_backward(): pair_tiles[:, :, :model_width].reshape(-1, head_count, head_width)  14.4 us
  transfers between devices with their start and end apart: 10, of which 3 were waited for; matrix products, arithmetic and copies ran while one was open for 14% of the time, Pallas kernels for 0%

profile of v1, /device:TPU:0, one launch (start us, length us, event | category | flops | bytes accessed | tf_op | source)
XLA Modules:
  0.0 587.4 jit_solution(11026103215495468854)
XLA Ops:
  16.4 5.1 collective-permute-start.3
  50.4 6.0 %collective-permute-done = bf16[2,128,1024]{2,1,0:T(8,128)(2,1)} collective-permute-done((bf16[2,128,1024]{2,1,0:T(8,128)(2,1)}, bf16[2,128,1024]{2,1,0:T(8,128)(2,1)}, u32[]{:S(2)}, u32[]{:S(2)}) %collective-permute-start) | collective-permute-done | bytes 524320 | tf_op jit(solution)/shard_map/ppermute | solution.py:19
  63.9 7.0 %gather_fusion = bf16[32,128,1024]{2,1,0:T(8,128)(2,1)} fusion(bf16[12,128,1024]{2,1,0:T(8,128)(2,1)} %constant_dynamic-update-slice_fusion, s32[1024]{0:T(1024)S(1)} %pad_clamp_fusion), kind=kCustom, calls=%fused_computation.4 | custom fusion | bytes 16777344 | tf_op jit(solution)/shard_map/while/body/eval_jaxpr/jit(_take)/gather | solution.py:130
  70.9 7.5 %broadcast_select_fusion = bf16[4,8,128,1024]{3,2,1,0:T(8,128)(2,1)} fusion(bf16[4,8,128,1024]{3,2,1,0:T(8,128)(2,1)} %bitcast.111, pred[4,8]{1,0:T(4,128)(4,1)S(1)} %get-tuple-element.55), kind=kLoop, calls=%fused_computation.18 | loop fusion | flops 4194304 | bytes 16777248 | tf_op jit(solution)/shard_map/while/body/eval_jaxpr/jit(_take)/select_n | solution.py:130
  78.4 5.9 %fusion.74 = (bf16[4,8,128,512]{3,2,1,0:T(8,128)(2,1)}, bf16[4,8,128,512]{3,2,1,0:T(8,128)(2,1)}) fusion(bf16[4,8,128,1024]{3,2,1,0:T(8,128)(2,1)} %broadcast_select_fusion), kind=kLoop, calls=%fused_computation.171 | loop fusion | bytes 16777216 | tf_op jit(solution)/shard_map/while/body/eval_jaxpr/vmap()/slice | solution.py:28
  84.2 6.9 %reshape.576 = bf16[4,1024,4,128]{3,2,1,0:T(4,128)(2,1)} reshape(bf16[4,8,128,512]{3,2,1,0:T(8,128)(2,1)} %get-tuple-element.58) | data formatting | bytes 8388608 | tf_op jit(solution)/shard_map/while/body/eval_jaxpr/vmap()/reshape | solution.py:27
  91.2 7.5 %copy.96 = bf16[4,1024,4,128]{1,3,2,0:T(8,128)(2,1)} copy(bf16[4,1024,4,128]{3,2,1,0:T(4,128)(2,1)} %reshape.576) | data formatting | bytes 8388608 | tf_op jit(solution)/shard_map/while/body/eval_jaxpr/vmap()/reshape | solution.py:27
  98.7 6.9 %reshape.577 = bf16[4,1024,4,128]{3,2,1,0:T(4,128)(2,1)} reshape(bf16[4,8,128,512]{3,2,1,0:T(8,128)(2,1)} %get-tuple-element.57) | data formatting | bytes 8388608 | tf_op jit(solution)/shard_map/while/body/eval_jaxpr/vmap()/reshape | solution.py:28
  105.6 7.6 %copy.95 = bf16[4,1024,4,128]{1,3,2,0:T(8,128)(2,1)} copy(bf16[4,1024,4,128]{3,2,1,0:T(4,128)(2,1)} %reshape.577) | data formatting | bytes 8388608 | tf_op jit(solution)/shard_map/while/body/eval_jaxpr/vmap()/reshape | solution.py:28
  113.2 6.8 %fusion.77 = f32[4,4,128,1024]{3,2,1,0:T(8,128)} fusion(bf16[4,128,4,128]{1,3,2,0:T(8,128)(2,1)S(1)} %copy-done.3, bf16[4,1024,4,128]{1,3,2,0:T(8,128)(2,1)} %copy.95), kind=kOutput, calls=%fused_computation.174 | convolution fusion | flops 536870912 | bytes 13107200 | tf_op jit(solution)/shard_map/while/body/eval_jaxpr/vmap(qhd,khd->hqk)/dot_general | solution.py:45
  120.0 8.5 %fusion.76 = (f32[4,4,128]{2,1,0:T(4,128)S(1)}, f32[4,4,128,1024]{3,2,1,0:T(8,128)}) fusion(pred[4,1024]{1,0:T(4,128)(4,1)S(1)} %bitcast.123, bf16[4,128,4,128]{1,3,2,0:T(8,128)(2,1)S(1)} %copy-done.7, bf16[4,1024,4,128]{1,3,2,0:T(8,128)(2,1)} %copy.96), kind=kOutput, calls=%fused_computation.173 | convolution fusion | flops 545260544 | bytes 13119488 | tf_op jit(solution)/shard_map/while/body/eval_jaxpr/vmap()/sub | solution.py:38
  128.5 6.9 %fusion.30 = bf16[4,128,4,128]{1,3,2,0:T(8,128)(2,1)} fusion(bf16[4,1024,4,128]{1,3,2,0:T(8,128)(2,1)} %copy.95, f32[4,4,128,1024]{3,2,1,0:T(8,128)} %get-tuple-element.69, f32[4,4,128]{2,1,0:T(4,128)S(1)} %get-tuple-element.68), kind=kOutput, calls=%fused_computation.42 | convolution fusion | flops 541327360 | bytes 13115392 | tf_op jit(solution)/shard_map/while/body/eval_jaxpr/vmap(hqk,khd->qhd)/dot_general | solution.py:41
  135.5 4.0 convolution_bitcast_fusion
  139.6 23.7 %fusion.15 = f32[4,1024,4,128]{1,3,2,0:T(8,128)} fusion(bf16[4,128,4,128]{1,3,2,0:T(8,128)(2,1)S(1)} %copy-done.7, f32[4,4,128,1024]{3,2,1,0:T(8,128)} %fusion.77, f32[4,4,128,1024]{3,2,1,0:T(8,128)} %get-tuple-element.69, f32[4,4,128]{2,1,0:T(4,128)S(1)} %get-tuple-element.68), kind=kOutput, calls=%fused_computation.26 | convolution fusion | flops 551554048 | bytes 25698304 | tf_op jit(solution)/shard_map/while/body/eval_jaxpr/vmap(hqk,qhd->khd)/dot_general | solution.py:51
  163.3 9.9 %copy.89 = f32[4,1024,4,128]{3,2,1,0:T(4,128)} copy(f32[4,1024,4,128]{1,3,2,0:T(8,128)} %fusion.15) | data formatting | bytes 16777216 | tf_op jit(solution)/shard_map/while/body/eval_jaxpr/vmap(hqk,qhd->khd)/transpose | solution.py:51
  173.2 10.3 %concatenate.21 = f32[32,128,512]{2,1,0:T(8,128)} reshape(f32[4,1024,4,128]{3,2,1,0:T(4,128)} %copy.89) | data formatting | bytes 16777216 | tf_op jit(solution)/shard_map/while/body/eval_jaxpr/vmap()/concatenate | solution.py:57
  183.4 9.9 %copy.91 = f32[4,1024,4,128]{3,2,1,0:T(4,128)} copy(f32[4,1024,4,128]{1,3,2,0:T(8,128)} %convolution_bitcast_fusion) | data formatting | bytes 16777216 | tf_op jit(solution)/shard_map/while/body/eval_jaxpr/vmap(hqk,qhd->khd)/transpose | solution.py:52
  193.3 10.3 %concatenate.22 = f32[32,128,512]{2,1,0:T(8,128)} reshape(f32[4,1024,4,128]{3,2,1,0:T(4,128)} %copy.91) | data formatting | bytes 16777216 | tf_op jit(solution)/shard_map/while/body/eval_jaxpr/vmap()/concatenate | solution.py:57
  203.6 11.7 %pad_maximum_fusion = f32[32,128,1024]{2,1,0:T(8,128)} fusion(f32[32,128,512]{2,1,0:T(8,128)} %concatenate.22, f32[32,128,512]{2,1,0:T(8,128)} %concatenate.21), kind=kLoop, calls=%fused_computation.12 | loop fusion | flops 4194304 | bytes 33554432 | tf_op jit(solution)/shard_map/while/body/eval_jaxpr/vmap()/concatenate | solution.py:57
  218.7 35.9 %scatter_fusion = f32[12,128,1024]{2,1,0:T(8,128)} fusion(f32[12,128,1024]{2,1,0:T(8,128)} %broadcast_in_dim.161, s32[32]{0:T(128)S(1)} %fusion.61, f32[32,128,1024]{2,1,0:T(8,128)} %pad_maximum_fusion), kind=kCustom, calls=%fused_computation.5 | custom fusion | flops 4194304 | bytes 50331776 | tf_op jit(solution)/shard_map/while/body/eval_jaxpr/scatter-add | solution.py:134
  254.6 4.9 convert.25
  273.1 22.8 %fusion.33 = bf16[4,128,4,128]{1,3,2,0:T(8,128)(2,1)S(1)} fusion(bf16[4,1024,4,128]{1,3,2,0:T(8,128)(2,1)} %copy.96, f32[4,4,128,1024]{3,2,1,0:T(8,128)} %fusion.77, f32[4,4,128,1024]{3,2,1,0:T(8,128)} %get-tuple-element.69, f32[4,4,128]{2,1,0:T(4,128)S(1)} %get-tuple-element.68), kind=kOutput, calls=%fused_computation.43 | convolution fusion | flops 551816192 | bytes 21504000 | tf_op jit(solution)/shard_map/while/body/eval_jaxpr/vmap(hqk,khd->qhd)/dot_general | solution.py:48
  328.3 87.0 %all-reduce.7.cloned.1.call-done = (f32[512,1536]{1,0:T(8,128)}, f32[512,512]{1,0:T(8,128)}) async-done(((f32[512,1536]{1,0:T(8,128)}, f32[512,512]{1,0:T(8,128)}), (f32[512,1536]{1,0:T(8,128)}, f32[512,512]{1,0:T(8,128)})) %all-reduce.7.cloned.1.call-update) | async-done | bytes 4194320 | tf_op jit(solution)/shard_map/psum | solution.py:173
  419.9 155.7 %all-reduce.5.cloned.1.call-done = (f32[512,1536]{1,0:T(8,128)}, f32[512,512]{1,0:T(8,128)}) async-done(((f32[512,1536]{1,0:T(8,128)}, f32[512,512]{1,0:T(8,128)}), (f32[512,1536]{1,0:T(8,128)}, f32[512,512]{1,0:T(8,128)})) %all-reduce.5.cloned.1.call-update) | async-done | bytes 4194320 | tf_op jit(solution)/shard_map/psum | solution.py:172
  (153 shorter events, 104.2 us)
Async XLA Ops:
  7.2 3.7 copy-start
  7.2 408.1 %all-reduce.7.cloned.1.call-start = ((), (), s32[]{:S(2)}) async-start(), calls=%async_computation.1 | async-start | bytes 8388608 | tf_op jit(solution)/shard_map/psum | solution.py:173
  11.9 1.1 copy-start.5
  13.1 23.5 %copy-start.9 = (s32[32,8]{0,1:T(8,128)S(1)}, s32[32,8]{0,1:T(8,128)}, u32[]{:S(2)}) copy-start(s32[32,8]{0,1:T(8,128)} %param.13) | copy-start | bytes 3076
  16.4 45.6 %collective-permute-start.3 = (bf16[2,128,1024]{2,1,0:T(8,128)(2,1)}, bf16[2,128,1024]{2,1,0:T(8,128)(2,1)}, u32[]{:S(2)}, u32[]{:S(2)}) collective-permute-start(bf16[2,128,1024]{2,1,0:T(8,128)(2,1)} %broadcast_select_fusion.1), channel_id=1, source_target_pairs={{0,24},{4,28},{8,0},{12,4},{16,8},{20,12},{24,16},{28,20},{1,25},{... | collective-permute-start | bytes 1572872 | tf_op jit(solution)/shard_map/ppermute | solution.py:19
  24.9 35.3 %collective-permute-start.2 = (bf16[2,128,1024]{2,1,0:T(8,128)(2,1)}, bf16[2,128,1024]{2,1,0:T(8,128)(2,1)}, u32[]{:S(2)}, u32[]{:S(2)}) collective-permute-start(bf16[2,128,1024]{2,1,0:T(8,128)(2,1)} %broadcast_select_fusion.2), channel_id=1, source_target_pairs={{0,28},{4,0},{8,4},{12,8},{16,12},{20,16},{24,20},{28,24},{1,29},{... | collective-permute-start | bytes 1572872 | tf_op jit(solution)/shard_map/ppermute | solution.py:19
  30.2 28.1 %collective-permute-start.1 = (bf16[2,128,1024]{2,1,0:T(8,128)(2,1)}, bf16[2,128,1024]{2,1,0:T(8,128)(2,1)}, u32[]{:S(2)}, u32[]{:S(2)}) collective-permute-start(bf16[2,128,1024]{2,1,0:T(8,128)(2,1)} %broadcast_select_fusion.3), channel_id=1, source_target_pairs={{0,4},{4,8},{8,12},{12,16},{16,20},{20,24},{24,28},{28,0},{1,5},{5... | collective-permute-start | bytes 1572872 | tf_op jit(solution)/shard_map/ppermute | solution.py:19
  34.2 22.3 %collective-permute-start = (bf16[2,128,1024]{2,1,0:T(8,128)(2,1)}, bf16[2,128,1024]{2,1,0:T(8,128)(2,1)}, u32[]{:S(2)}, u32[]{:S(2)}) collective-permute-start(bf16[2,128,1024]{2,1,0:T(8,128)(2,1)} %broadcast_select_fusion.4), channel_id=1, source_target_pairs={{0,8},{4,12},{8,16},{12,20},{16,24},{20,28},{24,0},{28,4},{1,9},{5... | collective-permute-start | bytes 1572872 | tf_op jit(solution)/shard_map/ppermute | solution.py:19
  105.6 7.6 %copy-start.3 = (bf16[4,128,4,128]{1,3,2,0:T(8,128)(2,1)S(1)}, bf16[4,128,4,128]{1,3,2,0:T(8,128)(2,1)}, u32[]{:S(2)}) copy-start(bf16[4,128,4,128]{1,3,2,0:T(8,128)(2,1)} %copy.90) | copy-start | bytes 1572868
  113.2 6.8 %copy-start.7 = (bf16[4,128,4,128]{1,3,2,0:T(8,128)(2,1)S(1)}, bf16[4,128,4,128]{1,3,2,0:T(8,128)(2,1)}, u32[]{:S(2)}) copy-start(bf16[4,128,4,128]{1,3,2,0:T(8,128)(2,1)} %copy.88) | copy-start | bytes 1572868
  128.5 7.0 %copy-start.10 = (f32[4,4,128,1024]{3,2,1,0:T(8,128)S(1)}, f32[4,4,128,1024]{3,2,1,0:T(8,128)}, u32[]{:S(2)}) copy-start(f32[4,4,128,1024]{3,2,1,0:T(8,128)} %get-tuple-element.69) | copy-start | bytes 25165828
  259.6 3.2 copy-start.8
  266.8 33.9 %collective-permute-start.4 = (bf16[2,128,1024]{2,1,0:T(8,128)(2,1)}, bf16[2,128,1024]{2,1,0:T(8,128)(2,1)}, u32[]{:S(2)}, u32[]{:S(2)}) collective-permute-start(bf16[2,128,1024]{2,1,0:T(8,128)(2,1)} %get-tuple-element.62), channel_id=1, source_target_pairs={{0,24},{4,28},{8,0},{12,4},{16,8},{20,12},{24,16},{28,20},{1,25},{... | collective-permute-start | bytes 1572872 | tf_op jit(solution)/shard_map/ppermute | solution.py:19
  270.1 36.1 %collective-permute-start.5 = (bf16[2,128,1024]{2,1,0:T(8,128)(2,1)}, bf16[2,128,1024]{2,1,0:T(8,128)(2,1)}, u32[]{:S(2)}, u32[]{:S(2)}) collective-permute-start(bf16[2,128,1024]{2,1,0:T(8,128)(2,1)} %get-tuple-element.61), channel_id=1, source_target_pairs={{0,28},{4,0},{8,4},{12,8},{16,12},{20,16},{24,20},{28,24},{1,29},{... | collective-permute-start | bytes 1572872 | tf_op jit(solution)/shard_map/ppermute | solution.py:19
  271.6 40.1 %collective-permute-start.6 = (bf16[2,128,1024]{2,1,0:T(8,128)(2,1)}, bf16[2,128,1024]{2,1,0:T(8,128)(2,1)}, u32[]{:S(2)}, u32[]{:S(2)}) collective-permute-start(bf16[2,128,1024]{2,1,0:T(8,128)(2,1)} %get-tuple-element.60), channel_id=1, source_target_pairs={{0,4},{4,8},{8,12},{12,16},{16,20},{20,24},{24,28},{28,0},{1,5},{5... | collective-permute-start | bytes 1572872 | tf_op jit(solution)/shard_map/ppermute | solution.py:19
  272.1 26.1 %copy-start.1 = (bf16[1,512,512]{2,1,0:T(8,128)(2,1)S(1)}, bf16[1,512,512]{2,1,0:T(8,128)(2,1)}, u32[]{:S(2)}) copy-start(bf16[1,512,512]{2,1,0:T(8,128)(2,1)} %param.9) | copy-start | bytes 1572868
  272.1 45.2 %collective-permute-start.7 = (bf16[2,128,1024]{2,1,0:T(8,128)(2,1)}, bf16[2,128,1024]{2,1,0:T(8,128)(2,1)}, u32[]{:S(2)}, u32[]{:S(2)}) collective-permute-start(bf16[2,128,1024]{2,1,0:T(8,128)(2,1)} %get-tuple-element.59), channel_id=1, source_target_pairs={{0,8},{4,12},{8,16},{12,20},{16,24},{20,28},{24,0},{28,4},{1,9},{5... | collective-permute-start | bytes 1572872 | tf_op jit(solution)/shard_map/ppermute | solution.py:19
  324.6 1.0 copy-start.2
  328.2 247.4 %all-reduce.5.cloned.1.call-start = ((), (), s32[]{:S(2)}) async-start(), calls=%async_computation | async-start | bytes 8388608 | tf_op jit(solution)/shard_map/psum | solution.py:172
  416.3 2.3 copy-start.4
  575.6 3.9 copy-start.6
Sparse Core Ops, SparseCore 0:
  328.3 86.9 all-reduce.6
  419.0 156.5 all-reduce.4
